TPU v7x, 512 devices: a whole 4x4x16 slice. The times are simulated.
512 devices in a mesh: section: 32 (over z, x_hi), dp: 4 (over y), mp: 4 (over x_lo, core).
Axes of the slice: x: 4 (x_hi: 2, x_lo: 2; x = x_hi * 2 + x_lo), y: 4, z: 16, core: 2. Of those that a mesh axis runs over, the one named last changes fastest.
Arguments:
- memory: bfloat16 [4, 256, 2048], P('dp', None, ('section', 'mp')), may hold values from -18 to 18
- key_weight: bfloat16 [32, 2048, 2048], P('section', None, 'mp'), may hold values from -1 to 1
- value_weight: bfloat16 [32, 2048, 2048], P('section', None, 'mp'), may hold values from -0.125 to 0.125
- queries: bfloat16 [32, 4, 256, 2048], P('section', 'dp', None, 'mp'), may hold values from -1024 to 1024
- cotangent: bfloat16 [32, 4, 256, 2048], P('section', 'dp', None, 'mp'), may hold values from -6 to 6
- target_lengths: int32 [4], P('dp'), may hold values from 64 to 256, as said below
Outputs:
- context: bfloat16 [32, 4, 256, 2048], P('section', 'dp', None, 'mp')
- mem_grad: float32 [4, 256, 2048], P('dp', None, ('section', 'mp'))
Inputs may be any that keep to these rules, and one draw needn't show every extreme that they name: `target_lengths`: valid positions of a sequence come first; the last sequence is full.
All inputs are finite; a program needn't handle non-finite values.
Results may differ from a plain program's by a relative error of at most 0.013.
The roundings to bfloat16 on the way count: a program that leaves them out, or rounds other values in their place, can miss the bound.
Values may be sent and summed in bfloat16 or wider, within the bound.
No kernel may reach another device: no remote copies, remote signals or barrier semaphores. Data moves between devices by JAX's collectives and lax.ppermute only.
A program may use at most 64 MiB of HBM per device.

v0:
```python
import jax
import jax.numpy as jnp
from jax import lax
from jax.sharding import PartitionSpec as P

HEAD_DIM = 256


def on_device(memory, key_weight, value_weight, queries, cotangent, target_lengths):
    width = key_weight.shape[2]
    head_count = width // HEAD_DIM
    seq_rows = queries.shape[2]
    score_scale = HEAD_DIM ** (-0.5)
    mem_block = memory[0]
    mem_rows = mem_block.shape[0]
    full_memory = lax.all_gather(mem_block, ("section", "mp"), axis=1, tiled=True)
    token_total = lax.psum(target_lengths.astype(jnp.float32), "dp")
    slot_total = float(lax.axis_size("dp") * target_lengths.shape[0] * seq_rows)
    loss_weight = slot_total / token_total[0]
    valid = (jnp.arange(seq_rows, dtype=jnp.int32) < target_lengths[0]).astype(jnp.float32)
    layer_index = 0
    key_rows = jnp.dot(
        full_memory, key_weight[layer_index], preferred_element_type=jnp.float32
    ).astype(jnp.bfloat16)
    value_rows = jnp.dot(
        full_memory, value_weight[layer_index], preferred_element_type=jnp.float32
    ).astype(jnp.bfloat16)
    key_heads = key_rows.reshape(mem_rows, head_count, HEAD_DIM)
    value_heads = value_rows.reshape(mem_rows, head_count, HEAD_DIM)
    query_heads = queries[layer_index, 0].reshape(seq_rows, head_count, HEAD_DIM)
    scores = (
        jnp.einsum("thd,shd->hts", query_heads, key_heads, preferred_element_type=jnp.float32)
        * score_scale
    )
    attention = jax.nn.softmax(scores, axis=-1)
    attention_low = attention.astype(jnp.bfloat16)
    context = jnp.einsum(
        "hts,shd->thd", attention_low, value_heads, preferred_element_type=jnp.float32
    )
    context = (context * valid[:, None, None]).astype(jnp.bfloat16)
    contexts = [context.reshape(seq_rows, width)]
    weighted = cotangent[layer_index, 0].astype(jnp.float32) * (valid * loss_weight)[:, None]
    weighted = weighted.astype(jnp.bfloat16).reshape(seq_rows, head_count, HEAD_DIM)
    value_grad = jnp.einsum(
        "hts,thd->shd", attention_low, weighted, preferred_element_type=jnp.float32
    )
    value_grads = [value_grad.astype(jnp.bfloat16).reshape(mem_rows, width)]
    prob_grad = jnp.einsum(
        "thd,shd->hts", weighted, value_heads, preferred_element_type=jnp.float32
    )
    row_dot = jnp.sum(attention * prob_grad, axis=-1, keepdims=True)
    score_grad = (attention * (prob_grad - row_dot) * score_scale).astype(jnp.bfloat16)
    key_grad = jnp.einsum(
        "hts,thd->shd", score_grad, query_heads, preferred_element_type=jnp.float32
    )
    key_grads = [key_grad.astype(jnp.bfloat16).reshape(mem_rows, width)]
    contract_last = (((1,), (1,)), ((), ()))
    layer_index = 0
    key_part = key_weight[layer_index]
    value_part = value_weight[layer_index]
    running = lax.dot_general(
        key_part, key_grads[layer_index], contract_last, preferred_element_type=jnp.float32
    )
    running = running + lax.dot_general(
        value_part, value_grads[layer_index], contract_last, preferred_element_type=jnp.float32
    )
    own_part = lax.psum_scatter(running, ("section", "mp"), scatter_dimension=0, tiled=True)
    own_grad = own_part.T
    context_out = jnp.stack(contexts, axis=0)[:, None]
    return (context_out, own_grad[None])


def solution(mesh):
    return jax.shard_map(
        on_device,
        mesh=mesh,
        in_specs=(
            P("dp", None, ("section", "mp")),
            P("section", None, "mp"),
            P("section", None, "mp"),
            P("section", "dp", None, "mp"),
            P("section", "dp", None, "mp"),
            P("dp"),
        ),
        out_specs=(P("section", "dp", None, "mp"), P("dp", None, ("section", "mp"))),
        check_vma=False,
    )
```

profile of v0, /device:TPU:8, one launch (start us, length us, event | category | flops | bytes accessed | tf_op | source)
XLA Modules:
  0.0 430.5 jit_solution(5405295528852739863)
XLA Ops:
  7.2 0.0 copy-start
  7.2 0.0 all-gather.3.cloned.1.call-start
  7.2 0.7 all-gather.3.cloned.1.call-update
  7.9 0.0 reduce-scatter.4.cloned.1.call-start
  8.6 14.0 %psum.7 = f32[1]{0:T(128)} all-reduce(f32[1]{0:T(128)S(6)} %convert_element_type.59), channel_id=1, replica_groups=mesh['section'=32,'dp'=4,'mp'=4] {'dp'}, use_global_device_ids=true, to_apply=%region_2.0 | all-reduce | flops 1 | bytes 8 | tf_op jit(solution)/shard_map/psum | solution.py:17
  22.6 1.1 copy.41
  23.7 0.0 copy-start.2
  23.7 1.2 copy.38
  25.6 120.8 %all-gather.3.cloned.1.call-done = bf16[1,256,2048]{1,2,0:T(8,128)(2,1)} async-done(((bf16[1,256,16]{1,2,0:T(8,128)(2,1)}), bf16[1,256,2048]{1,2,0:T(8,128)(2,1)}) %all-gather.3.cloned.1.call-update) | async-done | bytes 1048592 | tf_op jit(solution)/shard_map/all_gather | solution.py:16
  146.4 0.0 copy-done
  146.4 1.9 fusion.22
  148.4 0.0 copy-start.6
  148.4 1.1 fusion.58
  149.5 2.6 fusion.19
  152.2 0.0 copy-start.4
  152.2 0.2 fusion.33
  152.4 0.5 copy-done.4
  152.9 1.6 convolution_convert_fusion
  154.5 1.6 fusion.18
  156.1 0.0 copy-start.1
  156.1 0.8 fusion.3
  156.9 0.8 copy-done.1
  157.7 2.1 fusion.2
  159.8 2.9 copy.39
  162.8 0.0 reduce-scatter.4.cloned.1.call-update
  162.8 0.9 copy-done.3
  163.7 0.1 copy-done.5
  163.8 1.5 fusion.25
  165.3 0.8 copy.32
  166.2 256.0 %reduce-scatter.4.cloned.1.call-done = f32[16,256]{1,0:T(8,128)} async-done(((f32[2048,256]{1,0:T(8,128)}), f32[16,256]{1,0:T(8,128)}) %reduce-scatter.4.cloned.1.call-update) | async-done | bytes 16400
  422.2 0.8 copy.40
  423.0 0.7 copy.33
  (6 shorter events, 0.0 us)
Async XLA Ops:
  7.2 139.3 %copy-start = (bf16[1,2048,512]{2,1,0:T(8,128)(2,1)S(1)}, bf16[1,2048,512]{2,1,0:T(8,128)(2,1)}, u32[]{:S(2)}) copy-start(bf16[1,2048,512]{2,1,0:T(8,128)(2,1)} %param.7) | copy-start | bytes 6291460
  7.2 139.2 %all-gather.3.cloned.1.call-start = ((), (), s32[]{:S(2)}) async-start(), calls=%async_computation.1 | async-start | bytes 1056768 | tf_op jit(solution)/shard_map/all_gather | solution.py:16
  7.9 414.3 %reduce-scatter.4.cloned.1.call-start = ((), (), s32[]{:S(2)}) async-start(), calls=%async_computation.2 | async-start | bytes 2113536
  23.7 124.7 %copy-start.2 = (bf16[1,1,256,512]{2,3,1,0:T(8,128)(2,1)}, bf16[1,1,256,512]{2,3,1,0:T(8,128)(2,1)S(1)}, u32[]{:S(2)}) copy-start(bf16[1,1,256,512]{2,3,1,0:T(8,128)(2,1)S(1)} %copy.41) | copy-start | bytes 786436
  148.4 3.8 copy-start.6
  152.2 0.7 copy-start.4
  156.1 1.6 copy-start.1
  162.7 0.9 copy-start.3
  162.8 1.0 copy-start.5
Sparse Core Ops, SparseCore 0:
  11.0 135.4 all-gather.2
  162.9 259.2 reduce-scatter.3
where the time goes:
time: 431 us
  waiting for transfers between devices  378 us (88%)
  between operations  15.5 us (4%)
  blocking collectives  14 us (3%)
  matrix products  13.5 us (3%)
  local copies, waits for them, and re-layouts  9.84 us (2%)
    unnamed x3, waiting for transfers between devices  257 us
    all_gather x1, waiting for transfers between devices, on_device(): lax.all_gather(mem_block, ('section', 'mp'), axis=1, tiled=True)  121 us
    psum x1, blocking collectives, on_device(): token_total = lax.psum(target_lengths.astype(jnp.float32), 'dp')  14 us
  transfers between devices with their start and end apart: 2, of which 2 were waited for; matrix products, arithmetic and copies ran while one was open for 1% of the time, Pallas kernels for 0%

commit v1 on v0

--- a/solution.py
+++ b/solution.py
@@ -13,7 +13,10 @@
     score_scale = HEAD_DIM ** (-0.5)
     mem_block = memory[0]
     mem_rows = mem_block.shape[0]
-    full_memory = lax.all_gather(mem_block, ("section", "mp"), axis=1, tiled=True)
+    z1 = lax.all_to_all(
+        jnp.stack([mem_block] * lax.axis_size(("section", "mp")), 0), ("section", "mp"), 0, 0
+    )
+    full_memory = jnp.concatenate(z1, 1)
     token_total = lax.psum(target_lengths.astype(jnp.float32), "dp")
     slot_total = float(lax.axis_size("dp") * target_lengths.shape[0] * seq_rows)
     loss_weight = slot_total / token_total[0]

time: 431 us -> 364 us (0.84)
  waiting for transfers between devices: 378 us -> 296 us
  starting transfers between devices: 0.08 us -> 20.4 us
  blocking collectives: 14 us -> 9.21 us
    all_gather x1 -> x0, waiting for transfers between devices: 121 us -> none  [on_device(): lax.all_gather(mem_block, ('section', 'mp'), axis=1, tiled=True)]
    all_to_all x0 -> x1, waiting for transfers between devices: none -> 41.9 us  [on_device(): lax.all_to_all(jnp.stack([mem_block] * lax.axis_size(('section', 'mp')),...]
    all_to_all x0 -> x1, starting transfers between devices: none -> 20.3 us  [on_device(): lax.all_to_all(jnp.stack([mem_block] * lax.axis_size(('section', 'mp')),...]
    psum x1, blocking collectives: 14 us -> 9.21 us  [on_device(): token_total = lax.psum(target_lengths.astype(jnp.float32), 'dp')]
    unnamed x3 -> x2, waiting for transfers between devices: 257 us -> 254 us
where the time goes in v1:
time: 364 us; the launch traced here: 363 us
  waiting for transfers between devices  296 us (81%)
  starting transfers between devices  20.4 us (6%)
  between operations  15.6 us (4%)
  matrix products  13.1 us (4%)
  local copies, waits for them, and re-layouts  9.34 us (3%)
  blocking collectives  9.21 us (3%)
    unnamed x2, waiting for transfers between devices  254 us
    all_to_all x1, waiting for transfers between devices, on_device(): lax.all_to_all(jnp.stack([mem_block] * lax.axis_size(('section', 'mp')),...  41.9 us
    all_to_all x1, starting transfers between devices, on_device(): lax.all_to_all(jnp.stack([mem_block] * lax.axis_size(('section', 'mp')),...  20.3 us
    psum x1, blocking collectives, on_device(): token_total = lax.psum(target_lengths.astype(jnp.float32), 'dp')  9.21 us
  transfers between devices with their start and end apart: 2, of which 2 were waited for; matrix products, arithmetic and copies ran while one was open for 1% of the time, Pallas kernels for 0%

profile of v1, /device:TPU:8, one launch (start us, length us, event | category | flops | bytes accessed | tf_op | source)
XLA Modules:
  0.0 363.1 jit_solution(3804488249603954803)
XLA Ops:
  7.2 0.0 copy-start
  7.2 0.0 copy-start.4
  7.2 0.0 copy-start.3
  7.2 1.9 stack.3
  9.1 20.3 %all-to-all-start = ((bf16[128,256,16]{1,2,0:T(8,128)(2,1)}), bf16[128,256,16]{1,2,0:T(8,128)(2,1)}, u32[]{:S(2)}, u32[]{:S(2)}) async-start(bf16[128,256,16]{1,2,0:T(8,128)(2,1)} %stack.3), calls=%async_computation | async-start | bytes 2097152 | tf_op jit(solution)/shard_map/all_to_all | solution.py:16
  29.5 0.0 reduce-scatter.4.cloned.1.call-start
  30.2 9.2 %psum.7 = f32[1]{0:T(128)} all-reduce(f32[1]{0:T(128)S(6)} %convert_element_type.59), channel_id=1, replica_groups=mesh['section'=32,'dp'=4,'mp'=4] {'dp'}, use_global_device_ids=true, to_apply=%region_2.0 | all-reduce | flops 1 | bytes 8 | tf_op jit(solution)/shard_map/psum | solution.py:20
  39.4 0.0 copy-done.4
  39.4 0.1 copy.55
  39.5 0.1 copy.52
  40.4 41.9 %all-to-all-done = bf16[128,256,16]{1,2,0:T(8,128)(2,1)} async-done(((bf16[128,256,16]{1,2,0:T(8,128)(2,1)}), bf16[128,256,16]{1,2,0:T(8,128)(2,1)}, u32[]{:S(2)}, u32[]{:S(2)}) %all-to-all-start) | async-done | bytes 1048608 | tf_op jit(solution)/shard_map/all_to_all | solution.py:16
  82.3 2.1 fusion.22
  84.4 2.0 fusion.19
  86.4 0.0 copy-start.7
  86.5 1.1 fusion.56
  87.6 0.2 fusion.31
  87.8 0.0 copy-done.7
  87.8 1.6 convolution_convert_fusion
  89.5 1.6 fusion.18
  91.1 0.0 copy-start.2
  91.1 0.8 fusion.3
  91.8 0.8 copy-done.2
  92.7 2.1 fusion.2
  94.7 2.9 copy.53
  97.7 0.0 reduce-scatter.4.cloned.1.call-update
  97.7 0.9 copy-done.6
  98.6 0.1 copy-done.8
  98.7 1.5 fusion.25
  100.2 0.8 copy.46
  101.1 253.7 %reduce-scatter.4.cloned.1.call-done = f32[16,256]{1,0:T(8,128)} async-done(((f32[2048,256]{1,0:T(8,128)}), f32[16,256]{1,0:T(8,128)}) %reduce-scatter.4.cloned.1.call-update) | async-done | bytes 16400
  354.8 0.8 copy.54
  355.6 0.7 copy.47
  (12 shorter events, 0.0 us)
Async XLA Ops:
  7.2 75.1 %copy-start = (bf16[1,2048,512]{2,1,0:T(8,128)(2,1)S(1)}, bf16[1,2048,512]{2,1,0:T(8,128)(2,1)}, u32[]{:S(2)}) copy-start(bf16[1,2048,512]{2,1,0:T(8,128)(2,1)} %param.7) | copy-start | bytes 6291460
  7.2 32.2 %copy-start.4 = (bf16[1,1,256,512]{3,2,1,0:T(8,128)(2,1)S(1)}, bf16[1,1,256,512]{3,2,1,0:T(8,128)(2,1)}, u32[]{:S(2)}) copy-start(bf16[1,1,256,512]{3,2,1,0:T(8,128)(2,1)} %param.9) | copy-start | bytes 786436
  7.2 32.3 %copy-start.3 = (bf16[1,1,256,512]{3,2,1,0:T(8,128)(2,1)S(1)}, bf16[1,1,256,512]{3,2,1,0:T(8,128)(2,1)}, u32[]{:S(2)}) copy-start(bf16[1,1,256,512]{3,2,1,0:T(8,128)(2,1)} %param.10) | copy-start | bytes 786436
  9.1 73.1 %all-to-all-start = ((bf16[128,256,16]{1,2,0:T(8,128)(2,1)}), bf16[128,256,16]{1,2,0:T(8,128)(2,1)}, u32[]{:S(2)}, u32[]{:S(2)}) async-start(bf16[128,256,16]{1,2,0:T(8,128)(2,1)} %stack.3), calls=%async_computation | async-start | bytes 2097152 | tf_op jit(solution)/shard_map/all_to_all | solution.py:16
  29.5 325.3 %reduce-scatter.4.cloned.1.call-start = ((), (), s32[]{:S(2)}) async-start(), calls=%async_computation.2 | async-start | bytes 2113536
  39.5 46.9 %copy-start.5 = (bf16[1,1,256,512]{2,3,1,0:T(8,128)(2,1)}, bf16[1,1,256,512]{2,3,1,0:T(8,128)(2,1)S(1)}, u32[]{:S(2)}) copy-start(bf16[1,1,256,512]{2,3,1,0:T(8,128)(2,1)S(1)} %copy.55) | copy-start | bytes 786436
  82.3 2.1 copy-start.1
  84.4 3.2 copy-start.9
  86.4 1.4 copy-start.7
  91.1 1.6 copy-start.2
  97.7 0.9 copy-start.6
  97.7 1.0 copy-start.8
Sparse Core Ops, SparseCore 0:
  97.8 256.8 reduce-scatter.3
